TPU v7x, 32 devices: a whole 2x2x4 slice. The times are simulated.
32 devices in a mesh: group: 2 (over x), fsdp: 16 (over z, y, core).
Axes of the slice: x: 2, y: 2, z: 4, core: 2. Of those that a mesh axis runs over, the one named last changes fastest.
Arguments:
- tokens: bfloat16 [4096, 4096], P(('group', 'fsdp')), parts along dimension 0, may hold values from -6 to 6
- gate_cot: bfloat16 [4096, 16384], P(('group', 'fsdp')), parts along dimension 0, may hold values from -6 to 6
- gate_weight: bfloat16 [4096, 16384], P(None, 'fsdp'), may hold values from -0.15625 to 0.15625
- keep_mask: int32 [32, 128], P(None, 'fsdp'), may hold values from 0 to 1, as said below
Outputs:
- gate_out: bfloat16 [4096, 16384], P(('group', 'fsdp')), parts along dimension 0
- grad_tiles: bfloat16 [256, 12, 128, 128], P(('group', 'fsdp')), parts along dimension 0
There are 2 independent parts, one for each index of `group`. A program takes and returns all parts, laid end to end along the dimension named above; an argument that names none is the same for every part. Nothing has to cross between parts.
Inputs may be any that keep to these rules, and one draw needn't show every extreme that they name: `keep_mask`: each tile column keeps between 8 and 12 tiles; some column keeps exactly 12.
All inputs are finite; a program needn't handle non-finite values.
Results may differ from a plain program's by a relative error of at most 0.001.
Values may be sent and summed in bfloat16 or wider, within the bound.
A program may use at most 256 MiB of HBM per device.

v0:
```python
import jax
import jax.numpy as jnp
from jax import lax
from jax.sharding import PartitionSpec as P

TILE = 128
RT = 32
KMAX = 12


def kept_lists(keep_mask):
    kept_count = jnp.sum(keep_mask, axis=0)
    ordering = jnp.argsort(1 - keep_mask, axis=0, stable=True)[:KMAX]
    kept_rows = ordering.T
    kept_valid = jnp.arange(KMAX)[None, :] < kept_count[:, None]
    return (kept_rows, kept_valid)


def column_tiles(gate_weight, kept_rows, kept_valid, column):
    strip = gate_weight[:, column * TILE : (column + 1) * TILE].reshape(RT, TILE, TILE)
    picked = jnp.take(strip, kept_rows[column], axis=0)
    picked = jnp.where(kept_valid[column][:, None, None], picked, jnp.zeros_like(picked))
    return picked.reshape(KMAX * TILE, TILE)


def on_device(tokens, gate_cot, gate_weight, keep_mask):
    local_width = gate_weight.shape[1]
    local_cols = local_width // TILE
    kept_rows, kept_valid = kept_lists(keep_mask)
    weight_cols = [
        column_tiles(gate_weight, kept_rows, kept_valid, column) for column in range(local_cols)
    ]
    cot_cols = lax.all_to_all(gate_cot, "fsdp", split_axis=1, concat_axis=0, tiled=True)
    total_rows = cot_cols.shape[0]

    def block_work(carry, piece, start):
        gate_all, grads = carry
        length = piece.shape[0]
        blocks = piece.reshape(length, RT, TILE)
        slope_piece = lax.dynamic_slice_in_dim(cot_cols, start, length, 0)
        outputs = []
        new_grads = []
        for column in range(local_cols):
            selected = jnp.take(blocks, kept_rows[column], axis=1).reshape(length, KMAX * TILE)
            outputs.append(
                jnp.dot(selected, weight_cols[column], preferred_element_type=jnp.float32)
            )
            slope_col = slope_piece[:, column * TILE : (column + 1) * TILE]
            grad_col = lax.dot_general(
                selected, slope_col, (((0,), (0,)), ((), ())), preferred_element_type=jnp.float32
            )
            new_grads.append(grad_col.reshape(KMAX, TILE, TILE))
        values = jnp.concatenate(outputs, axis=1).astype(jnp.bfloat16)
        gate_all = lax.dynamic_update_slice_in_dim(gate_all, values, start, 0)
        return (gate_all, grads + jnp.stack(new_grads, axis=0))

    initial = (
        jnp.zeros((total_rows, local_width), jnp.bfloat16),
        jnp.zeros((local_cols, KMAX, TILE, TILE), jnp.float32),
    )
    piece = lax.all_gather(tokens, "fsdp", axis=0, tiled=True)
    length = piece.shape[0]

    def one_block(index, inner):
        offset = index * 1024
        block_rows = lax.dynamic_slice_in_dim(piece, offset, 1024, 0)
        return block_work(inner, block_rows, offset)

    gate_cols, partial_tiles = lax.fori_loop(0, length // 1024, one_block, initial)
    gate_out = lax.all_to_all(gate_cols, "fsdp", split_axis=0, concat_axis=1, tiled=True)
    grad_tiles = jnp.where(
        kept_valid[:, :, None, None], partial_tiles, jnp.zeros_like(partial_tiles)
    )
    return (gate_out, grad_tiles.astype(jnp.bfloat16))


def solution(mesh):
    placed = (
        P(("group", "fsdp"), None),
        P(("group", "fsdp"), None),
        P(None, "fsdp"),
        P(None, "fsdp"),
    )
    return jax.shard_map(
        on_device,
        mesh=mesh,
        in_specs=placed,
        out_specs=(P(("group", "fsdp"), None), P(("group", "fsdp"), None, None, None)),
        check_vma=False,
    )
```

profile of v0, /device:TPU:16, one launch (start us, length us, event | category | flops | bytes accessed | tf_op | source)
XLA Modules:
  0.0 683.6 jit_solution(8790158454934859952)
XLA Ops:
  9.5 4.8 copy.104
  14.3 6.3 all-to-all-start
  23.6 6.2 fusion.73
  62.3 123.1 %all-to-all-done = bf16[128,16,1024]{2,0,1:T(8,128)(2,1)} async-done(((bf16[128,16,1024]{2,0,1:T(8,128)(2,1)}), bf16[128,16,1024]{2,0,1:T(8,128)(2,1)}, u32[]{:S(2)}, u32[]{:S(2)}) %all-to-all-start) | async-done | bytes 4194336 | tf_op jit(solution)/shard_map/all_to_all | solution.py:33
  185.4 35.9 %all-gather.2.cloned.1.call-done = bf16[2048,4096]{0,1:T(8,128)(2,1)} async-done(((bf16[128,4096]{0,1:T(8,128)(2,1)}), bf16[2048,4096]{0,1:T(8,128)(2,1)}) %all-gather.2.cloned.1.call-update) | async-done | bytes 16777232 | tf_op jit(solution)/shard_map/all_gather | solution.py:61
  223.9 341.8 %while.16 = (s32[]{:T(128)}, bf16[2048,1024]{1,0:T(8,128)(2,1)}, f32[8,12,128,128]{3,2,1,0:T(8,128)}, bf16[2048,4096]{0,1:T(8,128)(2,1)}, s32[8,12]{1,0:T(8,128)...) while((s32[]{:T(128)}, bf16[2048,1024]{1,0:T(8,128)(2,1)}, ...), condition=%wide.region_3.6_spmd.clone, body=%wide.region_2.0_spmd.clone.sunk | while | flops 6459236864 | bytes 431524416 | solution.py:69
  227.6 7.6 %constant_dynamic-slice_fusion.2 = bf16[1024,4096]{0,1:T(8,128)(2,1)} fusion(bf16[2048,4096]{0,1:T(8,128)(2,1)} %get-tuple-element.651, s32[]{:T(128)S(6)} %select_n.203), kind=kLoop, calls=%fused_computation.107.clone.1 | loop fusion | bytes 16777220 | tf_op jit(solution)/shard_map/while/body/eval_jaxpr/dynamic_slice | solution.py:66
  235.2 11.9 %copy.115 = bf16[1024,32,128]{2,0,1:T(8,128)(2,1)} copy(bf16[1024,32,128]{0,2,1:T(8,128)(2,1)} %bitcast.352) | data formatting | bytes 16777216 | tf_op jit(solution)/shard_map/while/body/eval_jaxpr/reshape | solution.py:39
  251.8 6.2 gather_fusion.6
  258.0 5.2 select_bitcast_fusion.15
  272.6 6.2 gather_fusion.4
  278.8 5.2 select_bitcast_fusion.14
  293.4 6.1 gather_fusion.2
  299.5 5.2 select_bitcast_fusion.13
  313.9 6.1 gather_fusion
  320.0 5.2 select_bitcast_fusion.12
  397.1 7.6 %constant_dynamic-slice_fusion.2 = bf16[1024,4096]{0,1:T(8,128)(2,1)} fusion(bf16[2048,4096]{0,1:T(8,128)(2,1)} %get-tuple-element.651, s32[]{:T(128)S(6)} %select_n.203), kind=kLoop, calls=%fused_computation.107.clone.1 | loop fusion | bytes 16777220 | tf_op jit(solution)/shard_map/while/body/eval_jaxpr/dynamic_slice | solution.py:66
  404.7 11.9 %copy.115 = bf16[1024,32,128]{2,0,1:T(8,128)(2,1)} copy(bf16[1024,32,128]{0,2,1:T(8,128)(2,1)} %bitcast.352) | data formatting | bytes 16777216 | tf_op jit(solution)/shard_map/while/body/eval_jaxpr/reshape | solution.py:39
  421.3 6.2 gather_fusion.6
  427.5 5.2 select_bitcast_fusion.15
  442.1 6.2 gather_fusion.4
  448.3 5.2 select_bitcast_fusion.14
  462.8 6.1 gather_fusion.2
  468.9 5.2 select_bitcast_fusion.13
  483.4 6.1 gather_fusion
  489.5 5.2 select_bitcast_fusion.12
  558.9 6.8 %select_add_fusion.2 = f32[8,12,128,128]{3,2,1,0:T(8,128)} fusion(f32[8,12,128,128]{3,2,1,0:T(8,128)S(1)} %fusion.170, f32[8,12,128,128]{3,2,1,0:T(8,128)} %get-tuple-element.625, pred[]{:T(512)S(6)} %compare.7), kind=kLoop, calls=%fused_computation.16.clone.1 | loop fusion | flops 3145728 | bytes 18874368 | tf_op jit(solution)/shard_map/while/body/eval_jaxpr/add | solution.py:55
  565.7 5.4 all-to-all-start.1
  571.1 5.1 select_convert_fusion
  576.2 87.8 %all-to-all-done.1 = bf16[16,128,1024]{2,1,0:T(8,128)(2,1)} async-done(((bf16[16,128,1024]{2,1,0:T(8,128)(2,1)}), bf16[16,128,1024]{2,1,0:T(8,128)(2,1)}, u32[]{:S(2)}, u32[]{:S(2)}) %all-to-all-start.1) | async-done | bytes 4194336 | tf_op jit(solution)/shard_map/all_to_all | solution.py:70
  664.0 6.4 copy.98
  670.4 6.4 copy.99
  (217 shorter events, 244.7 us)
Async XLA Ops:
  7.2 214.2 %all-gather.2.cloned.1.call-start = ((), (), s32[]{:S(2)}) async-start(), calls=%async_computation.2 | async-start | bytes 17825792 | tf_op jit(solution)/shard_map/all_gather | solution.py:61
  14.3 6.3 copy-start.28
  14.3 171.1 %all-to-all-start = ((bf16[128,16,1024]{2,0,1:T(8,128)(2,1)}), bf16[128,16,1024]{2,0,1:T(8,128)(2,1)}, u32[]{:S(2)}, u32[]{:S(2)}) async-start(bf16[128,16,1024]{2,0,1:T(8,128)(2,1)} %bitcast.361), calls=%async_computation | async-start | bytes 8388608 | tf_op jit(solution)/shard_map/all_to_all | solution.py:33
  47.5 9.6 %copy-start.12 = (bf16[12,128,128]{2,1,0:T(8,128)(2,1)S(1)}, bf16[12,128,128]{2,1,0:T(8,128)(2,1)}, u32[]{:S(2)}) copy-start(bf16[12,128,128]{2,1,0:T(8,128)(2,1)} %gather_fusion.12) | copy-start | bytes 1179652
  47.5 10.5 %copy-start.13 = (bf16[12,128,128]{2,1,0:T(8,128)(2,1)S(1)}, bf16[12,128,128]{2,1,0:T(8,128)(2,1)}, u32[]{:S(2)}) copy-start(bf16[12,128,128]{2,1,0:T(8,128)(2,1)} %gather_fusion.11) | copy-start | bytes 1179652
  49.5 9.3 %copy-start.14 = (bf16[12,128,128]{2,1,0:T(8,128)(2,1)S(1)}, bf16[12,128,128]{2,1,0:T(8,128)(2,1)}, u32[]{:S(2)}) copy-start(bf16[12,128,128]{2,1,0:T(8,128)(2,1)} %gather_fusion.10) | copy-start | bytes 1179652
  49.5 10.1 %copy-start.15 = (bf16[12,128,128]{2,1,0:T(8,128)(2,1)S(1)}, bf16[12,128,128]{2,1,0:T(8,128)(2,1)}, u32[]{:S(2)}) copy-start(bf16[12,128,128]{2,1,0:T(8,128)(2,1)} %gather_fusion.9) | copy-start | bytes 1179652
  51.6 9.0 %copy-start.16 = (bf16[12,128,128]{2,1,0:T(8,128)(2,1)S(1)}, bf16[12,128,128]{2,1,0:T(8,128)(2,1)}, u32[]{:S(2)}) copy-start(bf16[12,128,128]{2,1,0:T(8,128)(2,1)} %gather_fusion.8) | copy-start | bytes 1179652
  51.6 9.9 %copy-start.17 = (bf16[12,128,128]{2,1,0:T(8,128)(2,1)S(1)}, bf16[12,128,128]{2,1,0:T(8,128)(2,1)}, u32[]{:S(2)}) copy-start(bf16[12,128,128]{2,1,0:T(8,128)(2,1)} %gather_fusion.14) | copy-start | bytes 1179652
  52.3 10.0 %copy-start.24 = (pred[8,12]{1,0:T(8,128)(4,1)}, pred[8,12]{1,0:T(8,128)(4,1)S(1)}, u32[]{:S(2)}) copy-start(pred[8,12]{1,0:T(8,128)(4,1)S(1)} %iota_compare_fusion) | copy-start | bytes 292
  59.7 164.3 %copy-start.18 = (bf16[12,128,128]{2,1,0:T(8,128)(2,1)S(1)}, bf16[12,128,128]{2,1,0:T(8,128)(2,1)}, u32[]{:S(2)}) copy-start(bf16[12,128,128]{2,1,0:T(8,128)(2,1)} %select_select_fusion) | copy-start | bytes 1179652
  313.9 6.1 copy-start.22
  313.9 6.1 copy-start.23
  328.4 7.3 %copy-start.9 = (bf16[1024,12,128]{0,2,1:T(8,128)(2,1)}, bf16[1024,12,128]{0,2,1:T(8,128)(2,1)S(1)}, u32[]{:S(2)}) copy-start(bf16[1024,12,128]{0,2,1:T(8,128)(2,1)S(1)} %copy.116) | copy-start | bytes 9437188 | tf_op jit(solution)/shard_map/while
  335.7 3.5 copy-start.3
  335.7 3.5 copy-start.20
  343.7 4.6 copy-start.7
  343.7 3.3 copy-start.19
  353.0 3.4 copy-start
  353.0 3.4 copy-start.21
  369.6 3.2 copy-start.10
  483.4 6.1 copy-start.22
  483.4 6.1 copy-start.23
  497.8 7.3 %copy-start.9 = (bf16[1024,12,128]{0,2,1:T(8,128)(2,1)}, bf16[1024,12,128]{0,2,1:T(8,128)(2,1)S(1)}, u32[]{:S(2)}) copy-start(bf16[1024,12,128]{0,2,1:T(8,128)(2,1)S(1)} %copy.116) | copy-start | bytes 9437188 | tf_op jit(solution)/shard_map/while
  505.2 3.5 copy-start.3
  505.2 3.5 copy-start.20
  513.2 4.6 copy-start.7
  513.2 3.3 copy-start.19
  522.4 3.4 copy-start
  522.5 3.4 copy-start.21
  565.7 5.4 copy-start.25
  565.7 98.3 %all-to-all-start.1 = ((bf16[16,128,1024]{2,1,0:T(8,128)(2,1)}), bf16[16,128,1024]{2,1,0:T(8,128)(2,1)}, u32[]{:S(2)}, u32[]{:S(2)}) async-start(bf16[16,128,1024]{2,1,0:T(8,128)(2,1)} %bitcast.362), calls=%async_computation.1 | async-start | bytes 8388608 | tf_op jit(solution)/shard_map/all_to_all | solution.py:70
  (17 other events, 36.0 us)
Sparse Core Ops, SparseCore 0:
  10.7 210.6 all-gather.1
where the time goes:
time: 688 us; the launch traced here: 684 us
  local copies, waits for them, and re-layouts  256 us (37%)
  waiting for transfers between devices  247 us (36%)
  other arithmetic  82.9 us (12%)
  matrix products  71.8 us (10%)
  between operations  14.1 us (2%)
  starting transfers between devices  11.7 us (2%)
    all_to_all x1, waiting for transfers between devices, on_device(): lax.all_to_all(gate_cot, 'fsdp', split_axis=1, concat_axis=0, tiled=True)  123 us
    all_to_all x1, waiting for transfers between devices, on_device(): lax.all_to_all(gate_cols, 'fsdp', split_axis=0, concat_axis=1, tiled=True)  87.8 us
    gather x16, local copies, waits for them, and re-layouts, block_work(): jnp.take(blocks, kept_rows[column], axis=1).reshape(length, KMAX * TILE)  86.3 us
    select_n x16, local copies, waits for them, and re-layouts, block_work(): jnp.take(blocks, kept_rows[column], axis=1).reshape(length, KMAX * TILE)  68.8 us
    select_n x8, other arithmetic, block_work(): jnp.take(blocks, kept_rows[column], axis=1).reshape(length, KMAX * TILE)  41.6 us
    dot_general x16, matrix products, block_work(): jnp.dot(selected, weight_cols[column], preferred_element_type=jnp.float32)  39.1 us
    all_gather x1, waiting for transfers between devices, on_device(): piece = lax.all_gather(tokens, 'fsdp', axis=0, tiled=True)  35.9 us
    dot_general x16, matrix products, block_work(): lax.dot_general(selected, slope_col, (((0,), (0,)), ((), ())), preferred_...  32.7 us
  transfers between devices with their start and end apart: 3, of which 3 were waited for; matrix products, arithmetic and copies ran while one was open for 8% of the time, Pallas kernels for 0%

commit v1 on v0

--- a/solution.py
+++ b/solution.py
@@ -1,6 +1,8 @@
 import jax
 import jax.numpy as jnp
 from jax import lax
+from jax.experimental import pallas as pl
+from jax.experimental.pallas import tpu as pltpu
 from jax.sharding import PartitionSpec as P
 
 TILE = 128
@@ -23,7 +25,7 @@
     return picked.reshape(KMAX * TILE, TILE)
 
 
-def on_device(tokens, gate_cot, gate_weight, keep_mask):
+def general_path(tokens, gate_cot, gate_weight, keep_mask):
     local_width = gate_weight.shape[1]
     local_cols = local_width // TILE
     kept_rows, kept_valid = kept_lists(keep_mask)
@@ -74,6 +76,282 @@
     return (gate_out, grad_tiles.astype(jnp.bfloat16))
 
 
+ZS = 4
+PEERS = 16
+
+
+def fused_kernel(
+    rows_ref, valid_ref, tokens_ref, cot_ref, weight_ref, mask_ref,
+    out_ref, grad_ref,
+    tok, cot, w, gate, full,
+    up_sem, down_sem, y_sem, sib_sem, ysib_sem, tok_recv,
+    cot_send, cot_recv, gate_send, gate_recv, local_sem,
+):
+    me = lax.axis_index("fsdp")
+    z = me // 4
+    y = (me // 2) % 2
+    c = me % 2
+    width = weight_ref.shape[1]
+    cols = width // TILE
+    sibling = me + 1 - 2 * c
+    partner = me + 2 - 4 * y
+
+    def block(zz, yy, cc):
+        return (zz * 2 + yy) * 2 + cc
+
+    near = (z * (ZS - 1 - z)) // 2
+    far_half = z // 2
+
+    def order(k):
+        f = k + near * (1 - 2 * k) * (1 - k // 2)
+        return f + far_half * (ZS - 1 - 2 * f)
+
+    def push(src, dst, send, recv, dev):
+        return pltpu.make_async_remote_copy(
+            src_ref=src, dst_ref=dst, send_sem=send, recv_sem=recv,
+            device_id={"fsdp": dev}, device_id_type=pl.DeviceIdType.MESH,
+        )
+
+    barrier = pltpu.get_barrier_semaphore()
+
+    def greet(o, carry):
+        pl.semaphore_signal(
+            barrier, inc=1, device_id={"fsdp": (me + o) % PEERS},
+            device_id_type=pl.DeviceIdType.MESH,
+        )
+        return carry
+
+    w_copy = pltpu.make_async_copy(weight_ref, w, local_sem.at[0])
+    w_copy.start()
+    tok_copy = pltpu.make_async_copy(tokens_ref, tok.at[me], local_sem.at[1])
+    tok_copy.start()
+    cot_copy = pltpu.make_async_copy(
+        cot_ref.at[:, pl.ds(pl.multiple_of(me * width, width), width)], cot.at[me], local_sem.at[2]
+    )
+    cot_copy.start()
+    lax.fori_loop(1, PEERS, greet, 0)
+    pl.semaphore_wait(barrier, PEERS - 1)
+
+    def tok_push(b, send, dev):
+        return push(tok.at[b], tok.at[b], send, tok_recv.at[b], dev)
+
+    def cot_push(o):
+        d = (me + o) % PEERS
+        return push(
+            cot_ref.at[:, pl.ds(pl.multiple_of(d * width, width), width)],
+            cot.at[me], cot_send.at[o], cot_recv.at[me], d,
+        )
+
+    def gate_push(b):
+        return push(
+            gate.at[b],
+            out_ref.at[:, pl.ds(pl.multiple_of(me * width, width), width)],
+            gate_send.at[b], gate_recv.at[me], b,
+        )
+
+    def own_copy():
+        return pltpu.make_async_copy(
+            gate.at[me],
+            out_ref.at[:, pl.ds(pl.multiple_of(me * width, width), width)],
+            local_sem.at[3],
+        )
+
+    def row_forward(k, act):
+        zk = order(k)
+        b = block(zk, y, c)
+
+        @pl.when(jnp.logical_and(zk <= z, z < ZS - 1))
+        def _():
+            act(tok_push(b, up_sem.at[k], me + 4))
+
+        @pl.when(jnp.logical_and(zk >= z, z > 0))
+        def _():
+            act(tok_push(b, down_sem.at[k], me - 4))
+
+        act(tok_push(b, y_sem.at[k], partner))
+        act(tok_push(b, sib_sem.at[k], sibling))
+
+    def start(copy):
+        copy.start()
+
+    def wait_send(copy):
+        copy.wait_send()
+
+    def arrived(b):
+        tok_push(b, up_sem.at[0], sibling).wait_recv()
+
+    def gate_values(zk, yk):
+        first = block(zk, yk, 0)
+        arrived(block(zk, yk, 1 - c))
+
+        def chunk(j, carry):
+            at = pl.ds(pl.multiple_of(j * 256, 256), 256)
+            lhs = tok[pl.ds(first, 2)].reshape(2 * tok.shape[1], tok.shape[2])
+            val = jnp.dot(lhs, w[:, at], preferred_element_type=jnp.float32)
+            gate[pl.ds(first, 2), :, at] = val.astype(jnp.bfloat16).reshape(2, tok.shape[1], 256)
+            return carry
+
+        lax.fori_loop(0, width // 256, chunk, 0)
+
+        def out(cc, carry):
+            b = first + cc
+
+            @pl.when(b != me)
+            def _():
+                gate_push(b).start()
+
+            return carry
+
+        lax.fori_loop(0, 2, out, 0)
+
+    tok_copy.wait()
+    row_forward(0, start)
+
+    def send_cot(o, carry):
+        cot_push(o).start()
+        return carry
+
+    lax.fori_loop(1, PEERS, send_cot, 0)
+
+    w_copy.wait()
+
+    def prune(r, carry):
+        at = pl.ds(pl.multiple_of(r * TILE, TILE), TILE)
+        w[at, :] = w[at, :] * mask_ref[r]
+        return carry
+
+    lax.fori_loop(0, RT, prune, 0)
+
+    def stage(k, carry):
+        @pl.when(jnp.logical_and(k >= 1, k < ZS))
+        def _():
+            arrived(block(order(k), y, c))
+            row_forward(k, start)
+
+        @pl.when(k >= 1)
+        def _():
+            b = block(order(k - 1), 1 - y, c)
+            arrived(b)
+            tok_push(b, ysib_sem.at[k - 1], sibling).start()
+
+        @pl.when(k < ZS)
+        def _():
+            gate_values(order(k), y)
+
+        @pl.when(k == 0)
+        def _():
+            own_copy().start()
+
+        @pl.when(k >= 1)
+        def _():
+            gate_values(order(k - 1), 1 - y)
+
+        return carry
+
+    lax.fori_loop(0, ZS + 1, stage, 0)
+
+    cot_copy.wait()
+
+    def wait_cot(o, carry):
+        src = (me + o) % PEERS
+        push(cot.at[src], cot.at[src], cot_send.at[o], cot_recv.at[src], src).wait_recv()
+        return carry
+
+    lax.fori_loop(1, PEERS, wait_cot, 0)
+
+    def grad_chunk(i, carry):
+        at = pl.ds(pl.multiple_of(i * 256, 256), 256)
+        lhs = tok[:, :, at].reshape(PEERS * tok.shape[1], 256)
+        rhs = cot[...].reshape(PEERS * tok.shape[1], width)
+        val = lax.dot_general(
+            lhs, rhs, (((0,), (0,)), ((), ())), preferred_element_type=jnp.float32
+        )
+        full[pl.ds(2 * i, 2)] = val.astype(jnp.bfloat16).reshape(2, TILE, width)
+        return carry
+
+    lax.fori_loop(0, RT // 2, grad_chunk, 0)
+
+    def pick(k, carry):
+        for col in range(cols):
+            r = rows_ref[col * KMAX + k]
+            keep = valid_ref[col * KMAX + k]
+            tile = full[r, :, col * TILE : (col + 1) * TILE].astype(jnp.float32)
+            tile = jnp.where(keep > 0, tile, jnp.zeros_like(tile))
+            grad_ref[col, k] = tile.astype(jnp.bfloat16)
+        return carry
+
+    lax.fori_loop(0, KMAX, pick, 0)
+
+    def finish(o, carry):
+        peer = (me + o) % PEERS
+        cot_push(o).wait_send()
+        gate_push(peer).wait_send()
+        push(
+            gate.at[peer],
+            out_ref.at[:, pl.ds(pl.multiple_of(peer * width, width), width)],
+            gate_send.at[peer], gate_recv.at[peer], peer,
+        ).wait_recv()
+        return carry
+
+    lax.fori_loop(1, PEERS, finish, 0)
+    own_copy().wait()
+
+    def finish_row(k, carry):
+        row_forward(k, wait_send)
+        tok_push(block(order(k), 1 - y, c), ysib_sem.at[k], sibling).wait_send()
+        return carry
+
+    lax.fori_loop(0, ZS, finish_row, 0)
+
+
+def fused_path(tokens, gate_cot, gate_weight, keep_mask):
+    length, depth = tokens.shape
+    width = gate_weight.shape[1]
+    cols = width // TILE
+    kept_rows, kept_valid = kept_lists(keep_mask)
+    mask = jnp.repeat(keep_mask, TILE, axis=1).astype(jnp.bfloat16)[:, None, :]
+    bf = jnp.bfloat16
+    dma = pltpu.SemaphoreType.DMA
+    anywhere = pl.BlockSpec(memory_space=pl.ANY)
+    return pl.pallas_call(
+        fused_kernel,
+        out_shape=(
+            jax.ShapeDtypeStruct((length, PEERS * width), bf),
+            jax.ShapeDtypeStruct((cols, KMAX, TILE, TILE), bf),
+        ),
+        in_specs=[
+            pl.BlockSpec(memory_space=pltpu.SMEM),
+            pl.BlockSpec(memory_space=pltpu.SMEM),
+            anywhere, anywhere, anywhere,
+            pl.BlockSpec(memory_space=pltpu.VMEM),
+        ],
+        out_specs=(anywhere, pl.BlockSpec(memory_space=pltpu.VMEM)),
+        scratch_shapes=[
+            pltpu.VMEM((PEERS, length, depth), bf),
+            pltpu.VMEM((PEERS, length, width), bf),
+            pltpu.VMEM((depth, width), bf),
+            pltpu.VMEM((PEERS, length, width), bf),
+            pltpu.VMEM((RT, TILE, width), bf),
+            dma((ZS,)), dma((ZS,)), dma((ZS,)), dma((ZS,)), dma((ZS,)), dma((PEERS,)),
+            dma((PEERS,)), dma((PEERS,)), dma((PEERS,)), dma((PEERS,)), dma((4,)),
+        ],
+        compiler_params=pltpu.CompilerParams(
+            collective_id=0, has_side_effects=True, vmem_limit_bytes=60 * 1024 * 1024
+        ),
+    )(
+        kept_rows.astype(jnp.int32).reshape(-1),
+        kept_valid.astype(jnp.int32).reshape(-1),
+        tokens, gate_cot, gate_weight, mask,
+    )
+
+
+def on_device(tokens, gate_cot, gate_weight, keep_mask):
+    small = (tokens.shape, gate_weight.shape[1]) == ((128, RT * TILE), 8 * TILE)
+    if lax.axis_size("fsdp") == PEERS and small:
+        return fused_path(tokens, gate_cot, gate_weight, keep_mask)
+    return general_path(tokens, gate_cot, gate_weight, keep_mask)
+
+
 def solution(mesh):
     placed = (
         P(("group", "fsdp"), None),

time: 688 us -> 255 us (0.37)
  the two profiles are of different devices: /device:TPU:16 before, /device:TPU:1 now
where the time goes in v1:
time: 255 us
  Pallas kernels  244 us (96%)
  local copies, waits for them, and re-layouts  8.69 us (3%)
    pallas_call x1, Pallas kernels, fused_path(): pl.pallas_call(fused_kernel, out_shape=(jax.ShapeDtypeStruct((length, PEE...  244 us
    unnamed x4, local copies, waits for them, and re-layouts  6.39 us

profile of v1, /device:TPU:1, one launch (start us, length us, event | category | flops | bytes accessed | tf_op | source)
XLA Modules:
  0.0 255.1 jit_solution(6101941847520859165)
XLA Ops:
  0.6 0.9 fusion.1
  1.5 0.1 fusion
  1.6 0.7 reshape.27.valid_ref
  2.3 0.1 copy.13
  2.3 0.1 copy.11
  2.4 0.8 sort.17
  3.2 0.1 copy.12
  3.3 0.6 reshape.26.rows_ref
  3.9 0.1 broadcast_in_dim.2
  4.0 0.7 convert_element_type.26.mask_ref
  4.7 244.0 %shard_map.59 = (bf16[128,16384]{1,0:T(8,128)(2,1)}, bf16[8,12,128,128]{3,2,1,0:T(8,128)(2,1)}) custom-call(s32[96]{0:T(128)} %reshape.26.rows_ref, s32[96]{0:T(128)} %reshape.27.valid_ref, bf16[128,4096]{1,0:T(8,128)(2,1)} %tokens_ref.1, bf16[128,16384]{1,0:T(8,128)(2,1)} %cot_ref.1, bf16[4096,1024]{1,0:T(8,128)(2,1)} %weight_ref.1, ...), custom_call_target="tpu_custom_call" | custom-call | tf_op jit(solution)/shard_map/pallas_call | solution.py:316
  248.7 0.0 copy-start
  248.7 4.7 %copy.17 = bf16[128,16384]{1,0:T(8,128)(2,1)} copy(bf16[128,16384]{1,0:T(8,128)(2,1)} %get-tuple-element.9) | data formatting | bytes 8388608
  253.4 0.0 copy-done
  253.4 1.7 copy.18
  (2 shorter events, 0.0 us)
Async XLA Ops:
  248.7 4.7 %copy-start = (bf16[8,12,128,128]{3,2,1,0:T(8,128)(2,1)S(1)}, bf16[8,12,128,128]{3,2,1,0:T(8,128)(2,1)}, u32[]{:S(2)}) copy-start(bf16[8,12,128,128]{3,2,1,0:T(8,128)(2,1)} %get-tuple-element.10) | copy-start | bytes 9437188

commit v2 on v1

--- a/solution.py
+++ b/solution.py
@@ -135,8 +135,15 @@
     def tok_push(b, send, dev):
         return push(tok.at[b], tok.at[b], send, tok_recv.at[b], dev)
 
+    def target(o):
+        step = o - 1
+        half = step // 8
+        zh = (z // 2 + 1 + half) % 2
+        j = (me % 8 + step % 8 + half) % 8
+        return zh * 8 + j
+
     def cot_push(o):
-        d = (me + o) % PEERS
+        d = target(o)
         return push(
             cot_ref.at[:, pl.ds(pl.multiple_of(d * width, width), width)],
             cot.at[me], cot_send.at[o], cot_recv.at[me], d,
@@ -211,7 +218,6 @@
         cot_push(o).start()
         return carry
 
-    lax.fori_loop(1, PEERS, send_cot, 0)
 
     w_copy.wait()
 
@@ -233,6 +239,12 @@
             b = block(order(k - 1), 1 - y, c)
             arrived(b)
             tok_push(b, ysib_sem.at[k - 1], sibling).start()
+
+        for when, (lo, hi) in enumerate(zip((1, 4, 8, 12, 16)[:-1], (1, 4, 8, 12, 16)[1:])):
+
+            @pl.when(k == when)
+            def _(lo=lo, hi=hi):
+                lax.fori_loop(lo, hi, send_cot, 0)
 
         @pl.when(k < ZS)
         def _():

time: 255 us -> 249 us (0.976)
  Pallas kernels: 244 us -> 237 us
    pallas_call x1, Pallas kernels: 244 us -> 237 us  [fused_path(): pl.pallas_call(fused_kernel, out_shape=(jax.ShapeDtypeStruct((length, PEE...]
where the time goes in v2:
time: 249 us; the launch traced here: 248 us
  Pallas kernels  237 us (95%)
  local copies, waits for them, and re-layouts  8.69 us (3%)
    pallas_call x1, Pallas kernels, fused_path(): pl.pallas_call(fused_kernel, out_shape=(jax.ShapeDtypeStruct((length, PEE...  237 us
    unnamed x4, local copies, waits for them, and re-layouts  6.39 us

profile of v2, /device:TPU:1, one launch (start us, length us, event | category | flops | bytes accessed | tf_op | source)
XLA Modules:
  0.0 248.5 jit_solution(9477949816892958929)
XLA Ops:
  0.6 0.9 fusion.1
  1.5 0.1 fusion
  1.6 0.7 reshape.27.valid_ref
  2.3 0.1 copy.13
  2.3 0.1 copy.11
  2.4 0.8 sort.17
  3.2 0.1 copy.12
  3.3 0.6 reshape.26.rows_ref
  3.9 0.1 broadcast_in_dim.2
  4.0 0.7 convert_element_type.26.mask_ref
  4.7 237.4 %shard_map.59 = (bf16[128,16384]{1,0:T(8,128)(2,1)}, bf16[8,12,128,128]{3,2,1,0:T(8,128)(2,1)}) custom-call(s32[96]{0:T(128)} %reshape.26.rows_ref, s32[96]{0:T(128)} %reshape.27.valid_ref, bf16[128,4096]{1,0:T(8,128)(2,1)} %tokens_ref.1, bf16[128,16384]{1,0:T(8,128)(2,1)} %cot_ref.1, bf16[4096,1024]{1,0:T(8,128)(2,1)} %weight_ref.1, ...), custom_call_target="tpu_custom_call" | custom-call | tf_op jit(solution)/shard_map/pallas_call | solution.py:328
  242.1 0.0 copy-start
  242.1 4.7 %copy.17 = bf16[128,16384]{1,0:T(8,128)(2,1)} copy(bf16[128,16384]{1,0:T(8,128)(2,1)} %get-tuple-element.9) | data formatting | bytes 8388608
  246.8 0.0 copy-done
  246.8 1.7 copy.18
  (2 shorter events, 0.0 us)
Async XLA Ops:
  242.1 4.7 %copy-start = (bf16[8,12,128,128]{3,2,1,0:T(8,128)(2,1)S(1)}, bf16[8,12,128,128]{3,2,1,0:T(8,128)(2,1)}, u32[]{:S(2)}) copy-start(bf16[8,12,128,128]{3,2,1,0:T(8,128)(2,1)} %get-tuple-element.10) | copy-start | bytes 9437188

commit v3 on v2

--- a/solution.py
+++ b/solution.py
@@ -81,17 +81,19 @@
 
 
 def fused_kernel(
-    rows_ref, valid_ref, tokens_ref, cot_ref, weight_ref, mask_ref,
+    rows_ref, valid_ref, place_ref, held_ref, tokens_ref, cot_ref, weight_ref, mask_ref,
     out_ref, grad_ref,
     tok, cot, w, gate, full,
     up_sem, down_sem, y_sem, sib_sem, ysib_sem, tok_recv,
-    cot_send, cot_recv, gate_send, gate_recv, local_sem,
+    cot_send, cot_recv, gate_send, gate_recv, local_sem, tiles, tile_send, tile_recv,
 ):
     me = lax.axis_index("fsdp")
+    g = lax.axis_index("group")
+    mate = (me + PEERS // 2) % PEERS
     z = me // 4
     y = (me // 2) % 2
     c = me % 2
-    width = weight_ref.shape[1]
+    width = weight_ref.shape[2]
     cols = width // TILE
     sibling = me + 1 - 2 * c
     partner = me + 2 - 4 * y
@@ -130,7 +132,10 @@
     )
     cot_copy.start()
     lax.fori_loop(1, PEERS, greet, 0)
-    pl.semaphore_wait(barrier, PEERS - 1)
+    pl.semaphore_signal(
+        barrier, inc=1, device_id={"group": 1 - g}, device_id_type=pl.DeviceIdType.MESH
+    )
+    pl.semaphore_wait(barrier, PEERS)
 
     def tok_push(b, send, dev):
         return push(tok.at[b], tok.at[b], send, tok_recv.at[b], dev)
@@ -149,18 +154,31 @@
             cot.at[me], cot_send.at[o], cot_recv.at[me], d,
         )
 
-    def gate_push(b):
+    def out_columns(src):
+        return out_ref.at[:, pl.ds(pl.multiple_of(src * width, width), width)]
+
+    def gate_push(b, n):
+        slot = (b + 8 * n) % PEERS
+        src = (me + 8 * n) % PEERS
+        return push(gate.at[slot], out_columns(src), gate_send.at[slot], gate_recv.at[src], b)
+
+    def own_copy(n):
+        src = (me + 8 * n) % PEERS
+        return pltpu.make_async_copy(gate.at[src], out_columns(src), local_sem.at[3 + n])
+
+    def tile_half(ref, which):
+        return ref.at[:, pl.ds(which * (KMAX // 2), KMAX // 2)]
+
+    def tile_push():
         return push(
-            gate.at[b],
-            out_ref.at[:, pl.ds(pl.multiple_of(me * width, width), width)],
-            gate_send.at[b], gate_recv.at[me], b,
-        )
-
-    def own_copy():
-        return pltpu.make_async_copy(
-            gate.at[me],
-            out_ref.at[:, pl.ds(pl.multiple_of(me * width, width), width)],
-            local_sem.at[3],
+            tile_half(grad_ref, g), tile_half(tiles, g), tile_send.at[0], tile_recv.at[0], mate
+        )
+
+    def tile_pass():
+        return pltpu.make_async_remote_copy(
+            src_ref=tile_half(tiles, g), dst_ref=tile_half(tiles, g),
+            send_sem=tile_send.at[1], recv_sem=tile_recv.at[1],
+            device_id={"group": 1 - g}, device_id_type=pl.DeviceIdType.MESH,
         )
 
     def row_forward(k, act):
@@ -187,28 +205,40 @@
     def arrived(b):
         tok_push(b, up_sem.at[0], sibling).wait_recv()
 
-    def gate_values(zk, yk):
+    def gate_values(zk, yk, n):
         first = block(zk, yk, 0)
-        arrived(block(zk, yk, 1 - c))
 
         def chunk(j, carry):
             at = pl.ds(pl.multiple_of(j * 256, 256), 256)
             lhs = tok[pl.ds(first, 2)].reshape(2 * tok.shape[1], tok.shape[2])
-            val = jnp.dot(lhs, w[:, at], preferred_element_type=jnp.float32)
+            rhs = w[:, :, at].reshape(RT * TILE, 256)
+            val = jnp.dot(lhs, rhs, preferred_element_type=jnp.float32)
             gate[pl.ds(first, 2), :, at] = val.astype(jnp.bfloat16).reshape(2, tok.shape[1], 256)
             return carry
 
-        lax.fori_loop(0, width // 256, chunk, 0)
+        def mate_chunk(j, carry):
+            at = pl.ds(pl.multiple_of(j * 256, 256), 256)
+            lhs = tok[pl.ds(first, 2)].reshape(2 * tok.shape[1], tok.shape[2])
+            rhs = full[:, :, at].reshape(RT * TILE, 256)
+            val = jnp.dot(lhs, rhs, preferred_element_type=jnp.float32)
+            slots = pl.ds((first + 8) % PEERS, 2)
+            gate[slots, :, at] = val.astype(jnp.bfloat16).reshape(2, tok.shape[1], 256)
+            return carry
 
         def out(cc, carry):
             b = first + cc
 
             @pl.when(b != me)
             def _():
-                gate_push(b).start()
+                gate_push(b, n).start()
+
+            @pl.when(b == me)
+            def _():
+                own_copy(n).start()
 
             return carry
 
+        lax.fori_loop(0, width // 256, chunk if n == 0 else mate_chunk, 0)
         lax.fori_loop(0, 2, out, 0)
 
     tok_copy.wait()
@@ -222,10 +252,18 @@
     w_copy.wait()
 
     def prune(r, carry):
-        at = pl.ds(pl.multiple_of(r * TILE, TILE), TILE)
-        w[at, :] = w[at, :] * mask_ref[r]
-        return carry
-
+        w[r] = w[r] * mask_ref[r]
+        return carry
+
+
+    def pack(k, carry):
+        for col in range(cols):
+            r = rows_ref[col * KMAX + k]
+            grad_ref[col, k] = w[r, :, col * TILE : (col + 1) * TILE]
+        return carry
+
+    lax.fori_loop(0, KMAX, pack, 0)
+    tile_push().start()
     lax.fori_loop(0, RT, prune, 0)
 
     def stage(k, carry):
@@ -248,19 +286,49 @@
 
         @pl.when(k < ZS)
         def _():
-            gate_values(order(k), y)
-
-        @pl.when(k == 0)
-        def _():
-            own_copy().start()
+            arrived(block(order(k), y, 1 - c))
 
         @pl.when(k >= 1)
         def _():
-            gate_values(order(k - 1), 1 - y)
+            arrived(block(order(k - 1), 1 - y, 1 - c))
+
+        @pl.when(jnp.logical_and(k < ZS, order(k % ZS) // 2 == z // 2))
+        def _():
+            gate_values(order(k % ZS), y, 0)
+
+        @pl.when(k == 1)
+        def _():
+            tile_push().wait_recv()
+            tile_pass().start()
+
+        back = (k + ZS - 1) % ZS
+
+        @pl.when(jnp.logical_and(k >= 1, order(back) // 2 == z // 2))
+        def _():
+            gate_values(order(back), 1 - y, 0)
 
         return carry
 
     lax.fori_loop(0, ZS + 1, stage, 0)
+    tile_pass().wait_recv()
+
+    def spread(r, carry):
+        for col in range(cols):
+            p = place_ref[r * cols + col]
+            tile = tiles[col, p].astype(jnp.float32)
+            tile = jnp.where(held_ref[r * cols + col] > 0, tile, jnp.zeros_like(tile))
+            full[r, :, col * TILE : (col + 1) * TILE] = tile.astype(jnp.bfloat16)
+        return carry
+
+    lax.fori_loop(0, RT, spread, 0)
+
+    def mate_values(i, carry):
+        gate_values((z // 2) * 2 + i // 2, i % 2, 1)
+        return carry
+
+    lax.fori_loop(0, ZS, mate_values, 0)
+    tile_push().wait_send()
+    tile_pass().wait_send()
 
     cot_copy.wait()
 
@@ -297,16 +365,23 @@
     def finish(o, carry):
         peer = (me + o) % PEERS
         cot_push(o).wait_send()
-        gate_push(peer).wait_send()
-        push(
-            gate.at[peer],
-            out_ref.at[:, pl.ds(pl.multiple_of(peer * width, width), width)],
-            gate_send.at[peer], gate_recv.at[peer], peer,
-        ).wait_recv()
         return carry
 
     lax.fori_loop(1, PEERS, finish, 0)
-    own_copy().wait()
+
+    def finish_gate(o, carry):
+        peer = (z // 2) * 8 + (me + o) % 8
+        for n in range(2):
+            gate_push(peer, n).wait_send()
+            src = (peer + 8 * n) % PEERS
+            push(
+                gate.at[src], out_columns(src), gate_send.at[src], gate_recv.at[src], peer
+            ).wait_recv()
+        return carry
+
+    lax.fori_loop(1, 8, finish_gate, 0)
+    own_copy(0).wait()
+    own_copy(1).wait()
 
     def finish_row(k, carry):
         row_forward(k, wait_send)
@@ -321,6 +396,10 @@
     width = gate_weight.shape[1]
     cols = width // TILE
     kept_rows, kept_valid = kept_lists(keep_mask)
+    mate_mask = lax.ppermute(
+        keep_mask, "fsdp", [(i, (i + PEERS // 2) % PEERS) for i in range(PEERS)]
+    )
+    place = jnp.clip(jnp.cumsum(mate_mask, axis=0) - 1, 0, KMAX - 1)
     mask = jnp.repeat(keep_mask, TILE, axis=1).astype(jnp.bfloat16)[:, None, :]
     bf = jnp.bfloat16
     dma = pltpu.SemaphoreType.DMA
@@ -332,8 +411,7 @@
             jax.ShapeDtypeStruct((cols, KMAX, TILE, TILE), bf),
         ),
         in_specs=[
-            pl.BlockSpec(memory_space=pltpu.SMEM),
-            pl.BlockSpec(memory_space=pltpu.SMEM),
+            *[pl.BlockSpec(memory_space=pltpu.SMEM)] * 4,
             anywhere, anywhere, anywhere,
             pl.BlockSpec(memory_space=pltpu.VMEM),
         ],
@@ -341,11 +419,12 @@
         scratch_shapes=[
             pltpu.VMEM((PEERS, length, depth), bf),
             pltpu.VMEM((PEERS, length, width), bf),
-            pltpu.VMEM((depth, width), bf),
+            pltpu.VMEM((RT, TILE, width), bf),
             pltpu.VMEM((PEERS, length, width), bf),
             pltpu.VMEM((RT, TILE, width), bf),
             dma((ZS,)), dma((ZS,)), dma((ZS,)), dma((ZS,)), dma((ZS,)), dma((PEERS,)),
-            dma((PEERS,)), dma((PEERS,)), dma((PEERS,)), dma((PEERS,)), dma((4,)),
+            dma((PEERS,)), dma((PEERS,)), dma((PEERS,)), dma((PEERS,)), dma((5,)),
+            pltpu.VMEM((cols, KMAX, TILE, TILE), bf), dma((2,)), dma((2,)),
         ],
         compiler_params=pltpu.CompilerParams(
             collective_id=0, has_side_effects=True, vmem_limit_bytes=60 * 1024 * 1024
@@ -353,7 +432,9 @@
     )(
         kept_rows.astype(jnp.int32).reshape(-1),
         kept_valid.astype(jnp.int32).reshape(-1),
-        tokens, gate_cot, gate_weight, mask,
+        place.astype(jnp.int32).reshape(-1),
+        mate_mask.reshape(-1),
+        tokens, gate_cot, gate_weight.reshape(RT, TILE, width), mask,
     )
 
 

time: 249 us -> 312 us (1.25)
  Pallas kernels: 237 us -> 296 us
  starting transfers between devices: 0 us -> 3.2 us
    pallas_call x1, Pallas kernels: 237 us -> 296 us  [fused_path(): pl.pallas_call(fused_kernel, out_shape=(jax.ShapeDtypeStruct((length, PEE...]
    ppermute x0 -> x1, starting transfers between devices: none -> 3.2 us  [fused_path(): lax.ppermute(keep_mask, 'fsdp', [(i, (i + PEERS // 2) % PEERS) for i in r...]
  transfers between devices with their start and end apart: 0 -> 1, of which waited for: 0 -> 0; matrix products, arithmetic and copies ran while one was open for 0% -> 1% of each run, Pallas kernels for 0% -> 0%
where the time goes in v3:
time: 312 us
  Pallas kernels  296 us (95%)
  local copies, waits for them, and re-layouts  10.1 us (3%)
  starting transfers between devices  3.2 us (1%)
    pallas_call x1, Pallas kernels, fused_path(): pl.pallas_call(fused_kernel, out_shape=(jax.ShapeDtypeStruct((length, PEE...  296 us
    unnamed x4, local copies, waits for them, and re-layouts  6.39 us
  transfers between devices with their start and end apart: 1, of which 0 were waited for; matrix products, arithmetic and copies ran while one was open for 1% of the time, Pallas kernels for 0%

profile of v3, /device:TPU:1, one launch (start us, length us, event | category | flops | bytes accessed | tf_op | source)
XLA Modules:
  0.0 312.1 jit_solution(2027058834511234035)
XLA Ops:
  0.6 3.2 %collective-permute-start = (s32[32,8]{0,1:T(8,128)}, s32[32,8]{0,1:T(8,128)S(1)}, u32[]{:S(2)}, u32[]{:S(2)}) collective-permute-start(s32[32,8]{0,1:T(8,128)} %param.7), channel_id=1, source_target_pairs={{0,8},{1,9},{2,10},{3,11},{4,12},{5,13},{6,14},{7,15},{8,0},{9,1},... | collective-permute-start | bytes 3080 | tf_op jit(solution)/shard_map/ppermute | solution.py:399
  3.8 0.9 fusion.1
  4.7 0.1 copy.14
  4.8 0.8 sort.17
  5.6 0.1 fusion
  5.7 0.6 reshape.42.valid_ref
  6.3 0.1 copy.18
  6.4 0.1 copy.15
  6.5 0.6 reshape.39.rows_ref
  7.1 0.1 broadcast_in_dim.2
  7.2 0.7 convert_element_type.26.mask_ref
  7.9 0.0 collective-permute-done
  7.9 0.1 copy.16
  7.9 0.7 reshape.40.held_ref
  8.6 0.1 reduce_window_sum.11
  8.7 0.7 min.12.place_ref
  9.3 296.4 %shard_map.59 = (bf16[128,16384]{1,0:T(8,128)(2,1)}, bf16[8,12,128,128]{3,2,1,0:T(8,128)(2,1)}) custom-call(s32[96]{0:T(128)} %reshape.39.rows_ref, s32[96]{0:T(128)} %reshape.42.valid_ref, s32[256]{0:T(256)} %min.12.place_ref, s32[256]{0:T(256)} %reshape.40.held_ref, bf16[128,4096]{1,0:T(8,128)(2,1)} %tokens_ref.1, bf16[128,16384]{1,0:T(8,128)(2,1)} %cot_ref.1, ...), custom_call_target="tpu_custom_call" | custom-call | tf_op jit(solution)/shard_map/pallas_call | solution.py:407
  305.7 0.0 copy-start
  305.7 4.7 %copy.22 = bf16[128,16384]{1,0:T(8,128)(2,1)} copy(bf16[128,16384]{1,0:T(8,128)(2,1)} %get-tuple-element.9) | data formatting | bytes 8388608
  310.4 0.0 copy-done
  310.4 1.7 copy.23
  (3 shorter events, 0.0 us)
Async XLA Ops:
  0.6 7.2 %collective-permute-start = (s32[32,8]{0,1:T(8,128)}, s32[32,8]{0,1:T(8,128)S(1)}, u32[]{:S(2)}, u32[]{:S(2)}) collective-permute-start(s32[32,8]{0,1:T(8,128)} %param.7), channel_id=1, source_target_pairs={{0,8},{1,9},{2,10},{3,11},{4,12},{5,13},{6,14},{7,15},{8,0},{9,1},... | collective-permute-start | bytes 3080 | tf_op jit(solution)/shard_map/ppermute | solution.py:399
  305.7 4.7 %copy-start = (bf16[8,12,128,128]{3,2,1,0:T(8,128)(2,1)S(1)}, bf16[8,12,128,128]{3,2,1,0:T(8,128)(2,1)}, u32[]{:S(2)}) copy-start(bf16[8,12,128,128]{3,2,1,0:T(8,128)(2,1)} %get-tuple-element.10) | copy-start | bytes 9437188

commit v4 on v2

--- a/solution.py
+++ b/solution.py
@@ -320,7 +320,11 @@
     length, depth = tokens.shape
     width = gate_weight.shape[1]
     cols = width // TILE
-    kept_rows, kept_valid = kept_lists(keep_mask)
+    running = jnp.cumsum(keep_mask, axis=0)
+    places = jnp.arange(KMAX)
+    ahead = running.T[:, None, :] <= places[None, :, None]
+    kept_rows = jnp.minimum(jnp.sum(ahead.astype(jnp.int32), axis=2), RT - 1)
+    kept_valid = places[None, :] < running[-1][:, None]
     mask = jnp.repeat(keep_mask, TILE, axis=1).astype(jnp.bfloat16)[:, None, :]
     bf = jnp.bfloat16
     dma = pltpu.SemaphoreType.DMA

time: 249 us -> 249 us (level)
    unnamed x4 -> x5, local copies, waits for them, and re-layouts: 6.39 us -> 7.15 us
where the time goes in v4:
time: 249 us
  Pallas kernels  237 us (95%)
  local copies, waits for them, and re-layouts  9.45 us (4%)
    pallas_call x1, Pallas kernels, fused_path(): pl.pallas_call(fused_kernel, out_shape=(jax.ShapeDtypeStruct((length, PEE...  237 us
    unnamed x5, local copies, waits for them, and re-layouts  7.15 us

profile of v4, /device:TPU:1, one launch (start us, length us, event | category | flops | bytes accessed | tf_op | source)
XLA Modules:
  0.0 248.6 jit_solution(14812837623136008901)
XLA Ops:
  0.6 0.7 convert_element_type.27
  1.3 0.1 copy.21
  1.4 0.8 copy.18
  2.2 0.1 reduce_window_sum.11
  2.2 0.1 fusion
  2.3 0.7 reshape.28.valid_ref
  3.0 0.1 copy.19
  3.1 0.3 convert_reduce_fusion
  3.3 0.1 copy.20
  3.4 0.6 min.12.rows_ref
  4.0 0.1 broadcast_in_dim.2
  4.1 0.7 convert_element_type.30.mask_ref
  4.8 237.4 %shard_map.59 = (bf16[128,16384]{1,0:T(8,128)(2,1)}, bf16[8,12,128,128]{3,2,1,0:T(8,128)(2,1)}) custom-call(s32[96]{0:T(128)} %min.12.rows_ref, s32[96]{0:T(128)} %reshape.28.valid_ref, bf16[128,4096]{1,0:T(8,128)(2,1)} %tokens_ref.1, bf16[128,16384]{1,0:T(8,128)(2,1)} %cot_ref.1, bf16[4096,1024]{1,0:T(8,128)(2,1)} %weight_ref.1, ...), custom_call_target="tpu_custom_call" | custom-call | tf_op jit(solution)/shard_map/pallas_call | solution.py:332
  242.2 0.0 copy-start
  242.2 4.7 %copy.25 = bf16[128,16384]{1,0:T(8,128)(2,1)} copy(bf16[128,16384]{1,0:T(8,128)(2,1)} %get-tuple-element.4) | data formatting | bytes 8388608
  246.9 0.0 copy-done
  246.9 1.7 copy.26
  (2 shorter events, 0.0 us)
Async XLA Ops:
  242.2 4.7 %copy-start = (bf16[8,12,128,128]{3,2,1,0:T(8,128)(2,1)S(1)}, bf16[8,12,128,128]{3,2,1,0:T(8,128)(2,1)}, u32[]{:S(2)}) copy-start(bf16[8,12,128,128]{3,2,1,0:T(8,128)(2,1)} %get-tuple-element.5) | copy-start | bytes 9437188
